TPU v7x, 128 devices: a whole 4x4x4 slice. The times are simulated.
128 devices in a mesh: dp: 4 (over x), tensor: 32 (over y, z, core).
Axes of the slice: x: 4, y: 4, z: 4, core: 2. Of those that a mesh axis runs over, the one named last changes fastest.
Arguments:
- tokens: bfloat16 [16384, 2048], P(('dp', 'tensor')), may hold values from -6 to 6
- norm_gain: bfloat16 [2048], replicated, may hold values from 0.099609375 to 1.8984375
- routes: int32 [16384, 6], P(('dp', 'tensor')), may hold values from 0 to 31, all different within a row; in each aligned block of 128 rows (0 to 127, 128 to 255, ...) at most 32 rows name the same one
- route_gates: bfloat16 [16384, 6], P(('dp', 'tensor')), may hold values from 0.19921875 to 1
- lengths: int32 [24], replicated, may hold values from 1 to 1920, 16384 in all
- request_adapter: int32 [24], replicated, may hold values from 0 to 31
- adapter_slot: int32 [32], replicated, may hold values from 0 to 31, each once
- expert_gate: bfloat16 [32, 2048, 1408], P('tensor'), may hold values from -0.125 to 0.125
- expert_up: bfloat16 [32, 2048, 1408], P('tensor'), may hold values from -0.125 to 0.125
- expert_down: bfloat16 [32, 1408, 2048], P('tensor'), may hold values from -0.15625 to 0.15625
- shared_gate: bfloat16 [2048, 1408], P(None, 'dp'), may hold values from -0.125 to 0.125
- shared_up_weight: bfloat16 [2048, 1408], P(None, 'dp'), may hold values from -0.125 to 0.125
- shared_down: bfloat16 [1408, 2048], P('dp'), may hold values from -0.15625 to 0.15625
- adapter_down: bfloat16 [32, 2048, 16], P('dp'), may hold values from -0.125 to 0.125
- adapter_up: bfloat16 [32, 16, 2048], P('dp'), may hold values from -1.5 to 1.5
- head_weight: bfloat16 [2048, 65536], P(None, ('dp', 'tensor')), may hold values from -0.375 to 0.375
Outputs:
- sublayer_out: bfloat16 [16384, 2048], P(('dp', 'tensor'))
- last_norm: float32 [24], replicated
- block_logit: float32 [24, 32], P(None, 'tensor')
Inputs may be any that keep to these rules, and one draw needn't show every extreme that they name: `routes`: in each aligned block of 128 rows (the rows of one device), no expert is named by more than 32 rows, a bound that some block reaches. The lengths sum to 16384; the largest is exactly 1920. Each position of the store appears once: adapter a is stored at position adapter_slot[a] of adapter_down and adapter_up.
All inputs are finite; a program needn't handle non-finite values.
Results may differ from a plain program's by a relative error of at most 0.0066.
Values may be sent and summed in bfloat16 or wider, within the bound.
A program may use at most 128 MiB of HBM per device.

v0:
```python
import jax
import jax.numpy as jnp
from jax import lax
from jax.sharding import PartitionSpec as P

CAP = 32


def apply_norm(tokens, norm_gain):
    values = tokens.astype(jnp.float32)
    scaled = lax.rsqrt(jnp.mean(values * values, axis=-1, keepdims=True) + 1e-06)
    return (values * scaled * norm_gain.astype(jnp.float32)).astype(jnp.bfloat16)


def feed_forward(inputs, gate_mat, up_mat, down_mat):
    gate_portion = jnp.dot(inputs, gate_mat, preferred_element_type=jnp.float32)
    up_part = jnp.dot(inputs, up_mat, preferred_element_type=jnp.float32)
    hidden = (jax.nn.silu(gate_portion) * up_part).astype(jnp.bfloat16)
    return jnp.dot(hidden, down_mat, preferred_element_type=jnp.float32)


def token_slots(positions, lengths, request_adapter, adapter_slot):
    request_ends = jnp.cumsum(lengths)
    request = jnp.sum((request_ends[None, :] <= positions[:, None]).astype(jnp.int32), axis=1)
    request_pick = (
        request[:, None] == jnp.arange(request_adapter.shape[0], dtype=jnp.int32)[None, :]
    )
    adapter = jnp.sum(jnp.where(request_pick, request_adapter[None, :], 0), axis=1)
    adapter_pick = adapter[:, None] == jnp.arange(adapter_slot.shape[0], dtype=jnp.int32)[None, :]
    return jnp.sum(jnp.where(adapter_pick, adapter_slot[None, :], 0), axis=1)


def adapter_delta(inputs, slot_ids, down_store, up_store):
    held_count = down_store.shape[0]
    model_width = down_store.shape[1]
    rank_size = down_store.shape[2]
    flat_down = jnp.transpose(down_store, (1, 0, 2)).reshape(model_width, held_count * rank_size)
    low_rank = jnp.dot(inputs, flat_down, preferred_element_type=jnp.float32)
    low_rank = low_rank.reshape(inputs.shape[0], held_count, rank_size)
    keep_mask = slot_ids[:, None] == jnp.arange(held_count, dtype=jnp.int32)[None, :]
    low_rank = jnp.where(keep_mask[:, :, None], low_rank, 0.0).astype(jnp.bfloat16)
    low_rank = low_rank.reshape(inputs.shape[0], held_count * rank_size)
    flat_up = up_store.reshape(held_count * rank_size, up_store.shape[2])
    return jnp.dot(low_rank, flat_up, preferred_element_type=jnp.float32)


def local(
    tokens,
    norm_gain,
    routes,
    route_gates,
    lengths,
    request_adapter,
    adapter_slot,
    expert_gate,
    expert_up,
    expert_down,
    shared_gate,
    shared_up_weight,
    shared_down,
    adapter_down,
    adapter_up,
    head_weight,
):
    tok_rows = tokens.shape[0]
    model_width = tokens.shape[1]
    route_count = routes.shape[1]
    tensor_size = lax.axis_size("tensor")
    tensor_pos = lax.axis_index("tensor")
    data_pos = lax.axis_index("dp")
    local_experts = expert_gate.shape[0]
    all_experts = local_experts * tensor_size
    slot_range = jnp.arange(CAP, dtype=jnp.int32)
    normed = apply_norm(tokens, norm_gain)
    numbers = jnp.arange(all_experts, dtype=jnp.int32)
    route_hits = routes[:, :, None] == numbers[None, None, :]
    chosen = jnp.any(route_hits, axis=1)
    weight = jnp.sum(
        jnp.where(route_hits, route_gates[:, :, None], jnp.zeros((), jnp.bfloat16)), axis=1
    )
    slot_place = jnp.cumsum(chosen.astype(jnp.int32), axis=0) - 1
    pooled, pooled_routes = (
        lax.all_gather(normed, "tensor", axis=0, tiled=True),
        lax.all_gather(routes.astype(jnp.bfloat16), "tensor", axis=0, tiled=True),
    )
    pooled = pooled.reshape(tensor_size, tok_rows, model_width)
    source_routes = pooled_routes.astype(jnp.int32).reshape(tensor_size, tok_rows, route_count)
    own_numbers = tensor_pos * local_experts + jnp.arange(local_experts, dtype=jnp.int32)
    source_hits = source_routes[:, :, :, None] == own_numbers[None, None, None, :]
    source_chosen = jnp.any(source_hits, axis=2)
    source_place = jnp.cumsum(source_chosen.astype(jnp.int32), axis=1) - 1
    source_pick = source_chosen[:, :, :, None] & (
        source_place[:, :, :, None] == slot_range[None, None, None, :]
    )
    source_pick = jnp.where(source_pick, 1.0, 0.0).astype(jnp.bfloat16)
    incoming = jnp.einsum(
        "sijc,sid->sjcd", source_pick, pooled, preferred_element_type=jnp.float32
    ).astype(jnp.bfloat16)
    gate_portion = jnp.einsum(
        "secd,edf->secf", incoming, expert_gate, preferred_element_type=jnp.float32
    )
    up_part = jnp.einsum("secd,edf->secf", incoming, expert_up, preferred_element_type=jnp.float32)
    hidden = (jax.nn.silu(gate_portion) * up_part).astype(jnp.bfloat16)
    expert_out = jnp.einsum(
        "secf,efd->secd", hidden, expert_down, preferred_element_type=jnp.float32
    ).astype(jnp.bfloat16)
    returned_rows = lax.all_to_all(expert_out, "tensor", split_axis=0, concat_axis=0, tiled=True)
    returned_rows = returned_rows.reshape(all_experts, CAP, model_width)
    mixing_result = jnp.where(
        slot_place[:, :, None] == slot_range[None, None, :],
        weight[:, :, None],
        jnp.zeros((), jnp.bfloat16),
    )
    routed_output = jnp.einsum(
        "kbt,btw->kw", mixing_result, returned_rows, preferred_element_type=jnp.float32
    )
    own_base = (data_pos * tensor_size + tensor_pos) * tok_rows
    own_positions = own_base + jnp.arange(tok_rows, dtype=jnp.int32)
    peer_rows = lax.all_gather(normed, "dp", axis=0, tiled=True)
    shared_sum = lax.psum_scatter(
        feed_forward(peer_rows, shared_gate, shared_up_weight, shared_down),
        "dp",
        scatter_dimension=0,
        tiled=True,
    )
    own_slots = token_slots(own_positions, lengths, request_adapter, adapter_slot)
    store_down, store_up = (
        lax.all_gather(adapter_down, "dp", axis=0, tiled=True),
        lax.all_gather(adapter_up, "dp", axis=0, tiled=True),
    )
    summed = routed_output + shared_sum + adapter_delta(normed, own_slots, store_down, store_up)
    sublayer_out = summed.astype(jnp.bfloat16)
    request_ends = jnp.cumsum(lengths)
    last_pick = jnp.where(request_ends[:, None] - 1 == own_positions[None, :], 1.0, 0.0).astype(
        jnp.bfloat16
    )
    last_part = jnp.dot(last_pick, sublayer_out, preferred_element_type=jnp.float32)
    last_states = lax.psum(last_part, ("dp", "tensor"))
    last_norm = jnp.sqrt(jnp.sum(last_states * last_states, axis=1))
    logits = jnp.dot(
        last_states.astype(jnp.bfloat16), head_weight, preferred_element_type=jnp.float32
    )
    block_logit = lax.pmax(jnp.max(logits, axis=1), "dp")
    return (sublayer_out, last_norm, block_logit[:, None])


def solution(mesh):
    placed = (
        P(("dp", "tensor"), None),
        P(),
        P(("dp", "tensor"), None),
        P(("dp", "tensor"), None),
        P(),
        P(),
        P(),
        P("tensor", None, None),
        P("tensor", None, None),
        P("tensor", None, None),
        P(None, "dp"),
        P(None, "dp"),
        P("dp", None),
        P("dp", None, None),
        P("dp", None, None),
        P(None, ("dp", "tensor")),
    )
    return jax.shard_map(
        local,
        mesh=mesh,
        in_specs=placed,
        out_specs=(P(("dp", "tensor"), None), P(), P(None, "tensor")),
        check_vma=False,
    )
```

profile of v0, /device:TPU:0, one launch (start us, length us, event | category | flops | bytes accessed | tf_op | source)
XLA Modules:
  0.0 401.9 jit_solution(9235097486257809376)
XLA Ops:
  7.2 0.0 all-gather.7.cloned.1.call-start
  7.2 0.9 convert_element_type.84
  8.1 1.3 fusion.41
  9.4 2.0 fusion.43
  11.4 0.0 all-gather.7.cloned.1.call-update
  11.5 0.0 all-gather.5.cloned.1.call-start
  11.5 0.7 all-gather.5.cloned.1.call-update
  12.2 0.0 reduce-scatter.2.cloned.1.call-start
  12.3 32.6 %all-gather.7.cloned.1.call-done = bf16[512,2048]{1,0:T(8,128)(2,1)} async-done(((bf16[128,2048]{1,0:T(8,128)(2,1)}), bf16[512,2048]{1,0:T(8,128)(2,1)}) %all-gather.7.cloned.1.call-update) | async-done | bytes 2097168 | tf_op jit(solution)/shard_map/all_gather | solution.py:119
  44.9 3.8 fusion.82
  48.7 6.3 %fusion.32 = f32[512,2048]{1,0:T(8,128)} fusion(bf16[352,2048]{1,0:T(8,128)(2,1)S(1)} %copy-done.8, bf16[512,2048]{1,0:T(8,128)(2,1)} %all-gather.7.cloned.1.call-done, bf16[2048,352]{0,1:T(8,128)(2,1)} %param.27, f32[512,352]{0,1:T(8,128)} %fusion.82), kind=kOutput, calls=%fused_computation.29 | convolution fusion | flops 1477476352 | bytes 9895936 | tf_op jit(solution)/shard_map/dot_general | solution.py:19
  55.0 0.0 reduce-scatter.2.cloned.1.call-update
  55.0 0.0 all-gather.11.cloned.1.call-start
  55.1 1.0 copy-done.4
  56.0 1.1 copy.47
  57.2 24.6 %all_gather.15 = bf16[4096,6]{0,1:T(8,128)(2,1)S(1)} all-gather(bf16[128,6]{0,1:T(8,128)(2,1)S(1)} %convert_element_type.79), channel_id=1, replica_groups=mesh['dp'=4,'tensor'=32] {'tensor'}, dimensions={0}, use_global_device_ids=true | all-gather | bytes 50688 | tf_op jit(solution)/shard_map/all_gather | solution.py:84
  81.7 0.1 fusion.63
  81.8 0.3 reduce_window_sum.31
  82.1 38.3 %all-gather.5.cloned.1.call-done = bf16[4096,2048]{1,0:T(8,128)(2,1)} async-done(((bf16[128,2048]{1,0:T(8,128)(2,1)}), bf16[4096,2048]{1,0:T(8,128)(2,1)}) %all-gather.5.cloned.1.call-update) | async-done | bytes 16777232 | tf_op jit(solution)/shard_map/all_gather | solution.py:83
  120.4 8.1 %convolution_convert_fusion = bf16[32,32,2048]{2,1,0:T(8,128)(2,1)S(1)} fusion(bf16[32,128,2048]{2,1,0:T(8,128)(2,1)} %bitcast.109, s32[32,128]{1,0:T(8,128)S(1)} %broadcast_add_fusion.1, pred[32,128]{1,0:T(8,128)(4,1)S(1)} %bitcast.111), kind=kOutput, calls=%fused_computation.16 | convolution fusion | flops 539492352 | bytes 20992000 | tf_op jit(solution)/shard_map/sijc,sid->sjcd/dot_general | solution.py:96
  128.5 2.1 copy-done.1
  130.6 10.7 %fusion.3 = f32[32,32,1408]{2,1,0:T(8,128)} fusion(bf16[32,32,2048]{2,1,0:T(8,128)(2,1)S(1)} %convolution_convert_fusion, bf16[1,2048,1408]{2,1,0:T(8,128)(2,1)} %param.24), kind=kOutput, calls=%fused_computation.4 | convolution fusion | flops 5905580032 | bytes 15728640 | tf_op jit(solution)/shard_map/secd,edf->secf/dot_general | solution.py:102
  141.3 21.0 %convert_bitcast_fusion = bf16[32,1,32,2048]{3,2,1,0:T(8,128)(2,1)} fusion(bf16[1,1408,2048]{2,1,0:T(8,128)(2,1)} %param.25, f32[32,32,1408]{2,1,0:T(8,128)} %fusion.3, bf16[32,32,2048]{2,1,0:T(8,128)(2,1)} %copy-done.1, bf16[1,2048,1408]{2,1,0:T(8,128)(2,1)} %param.23), kind=kOutput, calls=%fused_computation.15 | convolution fusion | flops 11821907968 | bytes 25690112 | tf_op jit(solution)/shard_map/secf,efd->secd/dot_general | solution.py:104
  162.4 5.2 %all-to-all-start = ((bf16[32,1,32,2048]{3,2,1,0:T(8,128)(2,1)}), bf16[32,1,32,2048]{3,2,1,0:T(8,128)(2,1)}, u32[]{:S(2)}, u32[]{:S(2)}) async-start(bf16[32,1,32,2048]{3,2,1,0:T(8,128)(2,1)} %convert_bitcast_fusion), calls=%async_computation | async-start | bytes 8388608 | tf_op jit(solution)/shard_map/all_to_all | solution.py:107
  167.6 0.0 all-gather.9.cloned.1.call-start
  167.7 0.5 all-gather.9.cloned.1.call-update
  168.2 0.3 all-reduce.2.cloned.1.call-start
  168.5 0.1 copy.42
  168.6 0.2 reduce_window_sum.30
  168.8 0.1 copy.43
  168.8 0.1 copy.45
  168.9 0.1 reduce-window.7
  169.0 0.1 reduce.2
  169.1 0.1 convert_reduce_fusion
  169.2 0.1 select_reduce_fusion.1
  169.3 0.1 select_reduce_fusion
  169.5 0.0 reduce-scatter.2.cloned.1.call-done
  169.5 50.9 %all-to-all-done = bf16[32,1,32,2048]{3,2,1,0:T(8,128)(2,1)} async-done(((bf16[32,1,32,2048]{3,2,1,0:T(8,128)(2,1)}), bf16[32,1,32,2048]{3,2,1,0:T(8,128)(2,1)}, u32[]{:S(2)}, u32[]{:S(2)}) %all-to-all-start) | async-done | bytes 4194336 | tf_op jit(solution)/shard_map/all_to_all | solution.py:107
  220.4 4.3 %fusion.23 = f32[128,2048]{1,0:T(8,128)} fusion(f32[128,2048]{1,0:T(8,128)} %reduce-scatter.2.cloned.1.call-done, bf16[32,1,32,2048]{3,2,1,0:T(8,128)(2,1)} %all-to-all-done, s32[128,32]{0,1:T(8,128)S(1)} %copy.43, bf16[128,32]{0,1:T(8,128)(2,1)S(1)} %fusion.68), kind=kOutput, calls=%fused_computation.21 | convolution fusion | flops 537395200 | bytes 6316032 | tf_op jit(solution)/shard_map/kbt,btw->kw/dot_general | solution.py:114
  224.7 9.1 %all-gather.9.cloned.1.call-done = bf16[32,2048,16]{1,2,0:T(8,128)(2,1)} async-done(((bf16[8,2048,16]{1,2,0:T(8,128)(2,1)}), bf16[32,2048,16]{1,2,0:T(8,128)(2,1)}) %all-gather.9.cloned.1.call-update) | async-done | bytes 2097168 | tf_op jit(solution)/shard_map/all_gather | solution.py:128
  233.7 4.5 %fusion.26 = bf16[128,2048]{1,0:T(8,128)(2,1)S(1)} fusion(f32[128,2048]{1,0:T(8,128)} %fusion.23, bf16[32,16,2048]{2,0,1:T(8,128)(2,1)} %all-gather.11.cloned.1.call-done, bf16[32,16,2048]{2,1,0:T(8,128)(2,1)} %bitcast.110, bf16[128,2048]{1,0:T(8,128)(2,1)S(1)} %copy-done.2, pred[128,32]{0,1:T(8,128)(4,1)S(1)} %iota_compare_fusion.3), kind=kOutput, calls=%fused_computation.22 | convolution fusion | flops 537526272 | bytes 6295552 | tf_op jit(solution)/shard_map/dot_general | solution.py:44
  238.3 0.9 fusion.69
  239.2 0.0 all-reduce.2.cloned.1.call-update
  239.2 143.1 %all-reduce.2.cloned.1.call-done = f32[24,2048]{1,0:T(8,128)} async-done(((f32[24,2048]{1,0:T(8,128)}), f32[24,2048]{1,0:T(8,128)}) %all-reduce.2.cloned.1.call-update) | async-done | bytes 196624 | tf_op jit(solution)/shard_map/psum | solution.py:138
  382.3 1.4 convolution_reduce_fusion
  383.7 9.7 %pmax.7 = f32[24,1]{0,1:T(1,128)} all-reduce(f32[24,1]{0,1:T(1,128)S(1)} %bitcast.112), channel_id=1, replica_groups=mesh['dp'=4,'tensor'=32] {'dp'}, use_global_device_ids=true, to_apply=%region_14.15 | all-reduce | flops 24 | bytes 192 | tf_op jit(solution)/shard_map/pmax | solution.py:143
  393.5 1.1 multiply_reduce_fusion
  394.6 0.5 sqrt.3
  (33 shorter events, 0.2 us)
Async XLA Ops:
  7.2 375.2 %copy-start = (bf16[2048,512]{1,0:T(8,128)(2,1)S(1)}, bf16[2048,512]{1,0:T(8,128)(2,1)}, u32[]{:S(2)}) copy-start(bf16[2048,512]{1,0:T(8,128)(2,1)} %param.31) | copy-start | bytes 6291460
  7.2 41.5 %copy-start.8 = (bf16[352,2048]{1,0:T(8,128)(2,1)S(1)}, bf16[352,2048]{1,0:T(8,128)(2,1)}, u32[]{:S(2)}) copy-start(bf16[352,2048]{1,0:T(8,128)(2,1)} %param.28) | copy-start | bytes 4325380
  7.2 37.7 %all-gather.7.cloned.1.call-start = ((), (), s32[]{:S(2)}) async-start(), calls=%async_computation.3 | async-start | bytes 2621440 | tf_op jit(solution)/shard_map/all_gather | solution.py:119
  11.5 109.0 %all-gather.5.cloned.1.call-start = ((), (), s32[]{:S(2)}) async-start(), calls=%async_computation.2 | async-start | bytes 17301504 | tf_op jit(solution)/shard_map/all_gather | solution.py:83
  12.2 157.3 %reduce-scatter.2.cloned.1.call-start = ((), (), s32[]{:S(2)}) async-start(), calls=%async_computation.4 | async-start | bytes 5242880 | tf_op jit(solution)/shard_map/reduce_scatter | solution.py:120
  55.0 1.0 copy-start.4
  55.0 2.1 copy-start.5
  55.0 169.6 %all-gather.11.cloned.1.call-start = ((), (), s32[]{:S(2)}) async-start(), calls=%async_computation.6 | async-start | bytes 2621440 | tf_op jit(solution)/shard_map/all_gather | solution.py:129
  128.5 2.1 copy-start.1
  162.3 6.5 %copy-start.7 = (s32[24]{0:T(128)S(1)}, s32[24]{0:T(128)}, u32[]{:S(2)}) copy-start(s32[24]{0:T(128)} %param.20) | copy-start | bytes 292
  162.3 6.9 %copy-start.9 = (s32[24]{0:T(128)S(1)}, s32[24]{0:T(128)}, u32[]{:S(2)}) copy-start(s32[24]{0:T(128)} %param.21) | copy-start | bytes 292
  162.3 7.0 %copy-start.10 = (s32[32]{0:T(128)S(1)}, s32[32]{0:T(128)}, u32[]{:S(2)}) copy-start(s32[32]{0:T(128)} %param.22) | copy-start | bytes 388
  162.4 7.1 %copy-start.6 = (bf16[128,6]{0,1:T(8,128)(2,1)S(1)}, bf16[128,6]{0,1:T(8,128)(2,1)}, u32[]{:S(2)}) copy-start(bf16[128,6]{0,1:T(8,128)(2,1)} %param.19) | copy-start | bytes 4612
  162.4 58.0 %all-to-all-start = ((bf16[32,1,32,2048]{3,2,1,0:T(8,128)(2,1)}), bf16[32,1,32,2048]{3,2,1,0:T(8,128)(2,1)}, u32[]{:S(2)}, u32[]{:S(2)}) async-start(bf16[32,1,32,2048]{3,2,1,0:T(8,128)(2,1)} %convert_bitcast_fusion), calls=%async_computation | async-start | bytes 8388608 | tf_op jit(solution)/shard_map/all_to_all | solution.py:107
  167.6 66.1 %copy-start.2 = (bf16[128,2048]{1,0:T(8,128)(2,1)S(1)}, bf16[128,2048]{1,0:T(8,128)(2,1)}, u32[]{:S(2)}) copy-start(bf16[128,2048]{1,0:T(8,128)(2,1)} %fusion.43) | copy-start | bytes 1572868
  167.6 66.1 %all-gather.9.cloned.1.call-start = ((), (), s32[]{:S(2)}) async-start(), calls=%async_computation.5 | async-start | bytes 2621440 | tf_op jit(solution)/shard_map/all_gather | solution.py:128
  168.2 214.1 %all-reduce.2.cloned.1.call-start = ((), (), s32[]{:S(2)}) async-start(), calls=%async_computation.7 | async-start | bytes 393216 | tf_op jit(solution)/shard_map/psum | solution.py:138
  238.3 156.8 %copy-start.3 = (bf16[128,2048]{1,0:T(8,128)(2,1)}, bf16[128,2048]{1,0:T(8,128)(2,1)S(1)}, u32[]{:S(2)}) copy-start(bf16[128,2048]{1,0:T(8,128)(2,1)S(1)} %fusion.26) | copy-start | bytes 1572868
Sparse Core Ops, SparseCore 0:
  11.6 33.2 all-gather.6
  47.7 72.6 all-gather.4
  122.8 46.1 reduce-scatter.1
  170.7 30.5 all-gather.10
  202.9 30.8 all-gather.8
  239.3 142.9 all-reduce.1
where the time goes:
time: 402 us
  waiting for transfers between devices  275 us (68%)
  matrix products  61.1 us (15%)
  blocking collectives  34.3 us (9%)
  between operations  14.3 us (4%)
  other arithmetic  6.28 us (2%)
  starting transfers between devices  5.69 us (1%)
  local copies, waits for them, and re-layouts  4.94 us (1%)
    psum x1, waiting for transfers between devices, local(): last_states = lax.psum(last_part, ('dp', 'tensor'))  143 us
    all_to_all x1, waiting for transfers between devices, local(): lax.all_to_all(expert_out, 'tensor', split_axis=0, concat_axis=0, tiled=T...  50.9 us
    all_gather x1, waiting for transfers between devices, local(): lax.all_gather(normed, 'tensor', axis=0, tiled=True)  38.3 us
    all_gather x1, waiting for transfers between devices, local(): peer_rows = lax.all_gather(normed, 'dp', axis=0, tiled=True)  32.6 us
    all_gather x1, blocking collectives, local(): lax.all_gather(routes.astype(jnp.bfloat16), 'tensor', axis=0, tiled=True)  24.6 us
    dot_general x1, matrix products, local(): jnp.einsum('secf,efd->secd', hidden, expert_down, preferred_element_type=...  21 us
    dot_general x1, matrix products, local(): jnp.einsum('secd,edf->secf', incoming, expert_up, preferred_element_type=...  10.7 us
    pmax x1, blocking collectives, local(): block_logit = lax.pmax(jnp.max(logits, axis=1), 'dp')  9.75 us
  transfers between devices with their start and end apart: 7, of which 5 were waited for; matrix products, arithmetic and copies ran while one was open for 14% of the time, Pallas kernels for 0%

commit v1 on v0

--- a/solution.py
+++ b/solution.py
@@ -116,7 +116,9 @@
     )
     own_base = (data_pos * tensor_size + tensor_pos) * tok_rows
     own_positions = own_base + jnp.arange(tok_rows, dtype=jnp.int32)
-    peer_rows = lax.all_gather(normed, "dp", axis=0, tiled=True)
+    peer_rows = jnp.concatenate(
+        lax.all_to_all(jnp.stack([normed] * lax.axis_size("dp")), "dp", 0, 0), axis=0
+    )
     shared_sum = lax.psum_scatter(
         feed_forward(peer_rows, shared_gate, shared_up_weight, shared_down),
         "dp",

time: 402 us -> 361 us (0.90)
  waiting for transfers between devices: 275 us -> 199 us
  blocking collectives: 34.3 us -> 65.5 us
    all_gather x1, waiting for transfers between devices: 38.3 us -> 4.51 us  [local(): lax.all_gather(normed, 'tensor', axis=0, tiled=True)]
    all_gather x1 -> x0, waiting for transfers between devices: 32.6 us -> none  [local(): peer_rows = lax.all_gather(normed, 'dp', axis=0, tiled=True)]
    all_to_all x0 -> x1, blocking collectives: none -> 30.5 us  [local(): lax.all_to_all(jnp.stack([normed] * lax.axis_size('dp')), 'dp', 0, 0)]
    all_gather x1, waiting for transfers between devices: 9.08 us -> 0.01 us  [local(): lax.all_gather(adapter_down, 'dp', axis=0, tiled=True)]
  transfers between devices with their start and end apart: 7 -> 6, of which waited for: 5 -> 3; matrix products, arithmetic and copies ran while one was open for 14% -> 16% of each run, Pallas kernels for 0% -> 0%
where the time goes in v1:
time: 361 us; the launch traced here: 360 us
  waiting for transfers between devices  199 us (55%)
  blocking collectives  65.5 us (18%)
  matrix products  60.7 us (17%)
  between operations  15.4 us (4%)
  local copies, waits for them, and re-layouts  7.57 us (2%)
  other arithmetic  6.29 us (2%)
  starting transfers between devices  6.17 us (2%)
    psum x1, waiting for transfers between devices, local(): last_states = lax.psum(last_part, ('dp', 'tensor'))  143 us
    all_to_all x1, waiting for transfers between devices, local(): lax.all_to_all(expert_out, 'tensor', split_axis=0, concat_axis=0, tiled=T...  50.7 us
    all_to_all x1, blocking collectives, local(): lax.all_to_all(jnp.stack([normed] * lax.axis_size('dp')), 'dp', 0, 0)  30.5 us
    all_gather x1, blocking collectives, local(): lax.all_gather(routes.astype(jnp.bfloat16), 'tensor', axis=0, tiled=True)  25.2 us
    dot_general x1, matrix products, local(): jnp.einsum('secf,efd->secd', hidden, expert_down, preferred_element_type=...  21.1 us
    dot_general x1, matrix products, local(): jnp.einsum('secd,edf->secf', incoming, expert_up, preferred_element_type=...  10.4 us
    pmax x1, blocking collectives, local(): block_logit = lax.pmax(jnp.max(logits, axis=1), 'dp')  9.8 us
    dot_general x1, matrix products, local(): jnp.einsum('sijc,sid->sjcd', source_pick, pooled, preferred_element_type=...  8.18 us
  transfers between devices with their start and end apart: 6, of which 3 were waited for; matrix products, arithmetic and copies ran while one was open for 16% of the time, Pallas kernels for 0%

profile of v1, /device:TPU:0, one launch (start us, length us, event | category | flops | bytes accessed | tf_op | source)
XLA Modules:
  0.0 360.4 jit_solution(13782004751530897071)
XLA Ops:
  8.0 0.0 all-gather.4.cloned.1.call-start
  8.1 0.8 convert_element_type.84
  8.9 1.2 fusion.41
  10.1 2.1 fusion.43
  12.3 0.0 all-gather.4.cloned.1.call-update
  12.3 0.0 reduce-scatter.2.cloned.1.call-start
  12.3 1.3 stack.2
  13.6 30.5 %all_to_all.10 = bf16[4,128,2048]{2,1,0:T(8,128)(2,1)S(1)} all-to-all(bf16[4,128,2048]{2,1,0:T(8,128)(2,1)S(1)} %stack.2), channel_id=1, replica_groups=mesh['dp'=4,'tensor'=32] {'dp'}, dimensions={0} | all-to-all | bytes 4194304 | tf_op jit(solution)/shard_map/all_to_all | solution.py:120
  44.1 1.3 copy-done.3
  45.5 1.8 fusion.82
  47.3 8.1 %fusion.32 = f32[512,2048]{1,0:T(8,128)} fusion(bf16[352,2048]{1,0:T(8,128)(2,1)} %param.28, bf16[512,2048]{1,0:T(8,128)(2,1)} %bitcast.112, bf16[2048,352]{0,1:T(8,128)(2,1)} %param.27, f32[512,352]{0,1:T(8,128)} %fusion.82), kind=kOutput, calls=%fused_computation.29 | convolution fusion | flops 1477476352 | bytes 9895936 | tf_op jit(solution)/shard_map/dot_general | solution.py:19
  55.4 0.0 reduce-scatter.2.cloned.1.call-update
  55.5 0.0 all-gather.8.cloned.1.call-start
  55.5 1.0 copy-done.5
  56.5 1.1 copy.47
  57.6 0.0 all-gather.8.cloned.1.call-update
  57.6 25.2 %all_gather.12 = bf16[4096,6]{0,1:T(8,128)(2,1)S(1)} all-gather(bf16[128,6]{0,1:T(8,128)(2,1)S(1)} %convert_element_type.79), channel_id=1, replica_groups=mesh['dp'=4,'tensor'=32] {'tensor'}, dimensions={0}, use_global_device_ids=true | all-gather | bytes 50688 | tf_op jit(solution)/shard_map/all_gather | solution.py:84
  82.8 0.1 fusion.63
  82.9 0.3 reduce_window_sum.31
  83.2 4.5 %all-gather.4.cloned.1.call-done = bf16[4096,2048]{1,0:T(8,128)(2,1)} async-done(((bf16[128,2048]{1,0:T(8,128)(2,1)}), bf16[4096,2048]{1,0:T(8,128)(2,1)}) %all-gather.4.cloned.1.call-update) | async-done | bytes 16777232 | tf_op jit(solution)/shard_map/all_gather | solution.py:83
  87.7 8.2 %convolution_convert_fusion = bf16[32,32,2048]{2,1,0:T(8,128)(2,1)S(1)} fusion(bf16[32,128,2048]{2,1,0:T(8,128)(2,1)} %bitcast.110, s32[32,128]{1,0:T(8,128)S(1)} %broadcast_add_fusion.1, pred[32,128]{1,0:T(8,128)(4,1)S(1)} %bitcast.114), kind=kOutput, calls=%fused_computation.16 | convolution fusion | flops 539492352 | bytes 20992000 | tf_op jit(solution)/shard_map/sijc,sid->sjcd/dot_general | solution.py:96
  95.9 2.1 copy-done.1
  98.0 10.4 %fusion.3 = f32[32,32,1408]{2,1,0:T(8,128)} fusion(bf16[32,32,2048]{2,1,0:T(8,128)(2,1)S(1)} %convolution_convert_fusion, bf16[1,2048,1408]{2,1,0:T(8,128)(2,1)} %param.24), kind=kOutput, calls=%fused_computation.4 | convolution fusion | flops 5905580032 | bytes 15728640 | tf_op jit(solution)/shard_map/secd,edf->secf/dot_general | solution.py:102
  108.3 21.1 %convert_bitcast_fusion = bf16[32,1,32,2048]{3,2,1,0:T(8,128)(2,1)} fusion(bf16[1,1408,2048]{2,1,0:T(8,128)(2,1)} %param.25, f32[32,32,1408]{2,1,0:T(8,128)} %fusion.3, bf16[32,32,2048]{2,1,0:T(8,128)(2,1)} %copy-done.1, bf16[1,2048,1408]{2,1,0:T(8,128)(2,1)} %param.23), kind=kOutput, calls=%fused_computation.15 | convolution fusion | flops 11821907968 | bytes 25690112 | tf_op jit(solution)/shard_map/secf,efd->secd/dot_general | solution.py:104
  129.4 5.7 %all-to-all-start = ((bf16[32,1,32,2048]{3,2,1,0:T(8,128)(2,1)}), bf16[32,1,32,2048]{3,2,1,0:T(8,128)(2,1)}, u32[]{:S(2)}, u32[]{:S(2)}) async-start(bf16[32,1,32,2048]{3,2,1,0:T(8,128)(2,1)} %convert_bitcast_fusion), calls=%async_computation | async-start | bytes 8388608 | tf_op jit(solution)/shard_map/all_to_all | solution.py:107
  135.2 0.0 all-gather.6.cloned.1.call-start
  135.2 0.7 all-gather.6.cloned.1.call-update
  135.9 0.3 all-reduce.2.cloned.1.call-start
  136.2 0.1 copy.42
  136.3 0.2 reduce_window_sum.30
  136.5 0.1 copy.43
  136.6 0.1 copy.45
  136.7 0.1 reduce-window.7
  136.7 0.1 reduce.2
  136.8 0.1 convert_reduce_fusion
  136.9 0.1 select_reduce_fusion.1
  137.0 0.1 select_reduce_fusion
  137.2 0.0 reduce-scatter.2.cloned.1.call-done
  137.2 50.7 %all-to-all-done = bf16[32,1,32,2048]{3,2,1,0:T(8,128)(2,1)} async-done(((bf16[32,1,32,2048]{3,2,1,0:T(8,128)(2,1)}), bf16[32,1,32,2048]{3,2,1,0:T(8,128)(2,1)}, u32[]{:S(2)}, u32[]{:S(2)}) %all-to-all-start) | async-done | bytes 4194336 | tf_op jit(solution)/shard_map/all_to_all | solution.py:107
  187.9 4.2 %fusion.23 = f32[128,2048]{1,0:T(8,128)} fusion(f32[128,2048]{1,0:T(8,128)} %reduce-scatter.2.cloned.1.call-done, bf16[32,1,32,2048]{3,2,1,0:T(8,128)(2,1)} %all-to-all-done, s32[128,32]{0,1:T(8,128)S(1)} %copy.43, bf16[128,32]{0,1:T(8,128)(2,1)S(1)} %fusion.68), kind=kOutput, calls=%fused_computation.21 | convolution fusion | flops 537395200 | bytes 6316032 | tf_op jit(solution)/shard_map/kbt,btw->kw/dot_general | solution.py:114
  192.2 4.5 %fusion.26 = bf16[128,2048]{1,0:T(8,128)(2,1)S(1)} fusion(f32[128,2048]{1,0:T(8,128)} %fusion.23, bf16[32,16,2048]{2,0,1:T(8,128)(2,1)} %all-gather.8.cloned.1.call-done, bf16[32,16,2048]{2,1,0:T(8,128)(2,1)} %bitcast.113, bf16[128,2048]{1,0:T(8,128)(2,1)S(1)} %copy-done.2, pred[128,32]{0,1:T(8,128)(4,1)S(1)} %iota_compare_fusion.3), kind=kOutput, calls=%fused_computation.22 | convolution fusion | flops 537526272 | bytes 6295552 | tf_op jit(solution)/shard_map/dot_general | solution.py:44
  196.7 0.9 fusion.69
  197.6 0.0 all-reduce.2.cloned.1.call-update
  197.6 142.8 %all-reduce.2.cloned.1.call-done = f32[24,2048]{1,0:T(8,128)} async-done(((f32[24,2048]{1,0:T(8,128)}), f32[24,2048]{1,0:T(8,128)}) %all-reduce.2.cloned.1.call-update) | async-done | bytes 196624 | tf_op jit(solution)/shard_map/psum | solution.py:140
  340.5 1.4 convolution_reduce_fusion
  341.9 9.8 %pmax.7 = f32[24,1]{0,1:T(1,128)} all-reduce(f32[24,1]{0,1:T(1,128)S(1)} %bitcast.115), channel_id=1, replica_groups=mesh['dp'=4,'tensor'=32] {'dp'}, use_global_device_ids=true, to_apply=%region_14.15 | all-reduce | flops 24 | bytes 192 | tf_op jit(solution)/shard_map/pmax | solution.py:145
  351.7 1.1 multiply_reduce_fusion
  352.7 0.5 sqrt.3
  (34 shorter events, 0.1 us)
Async XLA Ops:
  8.0 332.5 %copy-start = (bf16[2048,512]{1,0:T(8,128)(2,1)S(1)}, bf16[2048,512]{1,0:T(8,128)(2,1)}, u32[]{:S(2)}) copy-start(bf16[2048,512]{1,0:T(8,128)(2,1)} %param.31) | copy-start | bytes 6291460
  8.0 79.7 %all-gather.4.cloned.1.call-start = ((), (), s32[]{:S(2)}) async-start(), calls=%async_computation.3 | async-start | bytes 17301504 | tf_op jit(solution)/shard_map/all_gather | solution.py:83
  10.1 35.3 %copy-start.9 = (bf16[2048,352]{0,1:T(8,128)(2,1)S(1)}, bf16[2048,352]{0,1:T(8,128)(2,1)}, u32[]{:S(2)}) copy-start(bf16[2048,352]{0,1:T(8,128)(2,1)} %param.26) | copy-start | bytes 4325380
  12.3 124.9 %reduce-scatter.2.cloned.1.call-start = ((), (), s32[]{:S(2)}) async-start(), calls=%async_computation.4 | async-start | bytes 5242880 | tf_op jit(solution)/shard_map/reduce_scatter | solution.py:122
  44.1 1.3 copy-start.3
  55.4 1.1 copy-start.5
  55.4 2.2 copy-start.6
  55.5 136.7 %all-gather.8.cloned.1.call-start = ((), (), s32[]{:S(2)}) async-start(), calls=%async_computation.6 | async-start | bytes 2621440 | tf_op jit(solution)/shard_map/all_gather | solution.py:131
  95.9 2.1 copy-start.1
  129.4 7.2 %copy-start.8 = (s32[24]{0:T(128)S(1)}, s32[24]{0:T(128)}, u32[]{:S(2)}) copy-start(s32[24]{0:T(128)} %param.20) | copy-start | bytes 292
  129.4 7.5 %copy-start.10 = (s32[24]{0:T(128)S(1)}, s32[24]{0:T(128)}, u32[]{:S(2)}) copy-start(s32[24]{0:T(128)} %param.21) | copy-start | bytes 292
  129.4 7.6 %copy-start.11 = (s32[32]{0:T(128)S(1)}, s32[32]{0:T(128)}, u32[]{:S(2)}) copy-start(s32[32]{0:T(128)} %param.22) | copy-start | bytes 388
  129.4 7.7 %copy-start.7 = (bf16[128,6]{0,1:T(8,128)(2,1)S(1)}, bf16[128,6]{0,1:T(8,128)(2,1)}, u32[]{:S(2)}) copy-start(bf16[128,6]{0,1:T(8,128)(2,1)} %param.19) | copy-start | bytes 4612
  129.4 58.5 %all-to-all-start = ((bf16[32,1,32,2048]{3,2,1,0:T(8,128)(2,1)}), bf16[32,1,32,2048]{3,2,1,0:T(8,128)(2,1)}, u32[]{:S(2)}, u32[]{:S(2)}) async-start(bf16[32,1,32,2048]{3,2,1,0:T(8,128)(2,1)} %convert_bitcast_fusion), calls=%async_computation | async-start | bytes 8388608 | tf_op jit(solution)/shard_map/all_to_all | solution.py:107
  135.2 57.0 %copy-start.2 = (bf16[128,2048]{1,0:T(8,128)(2,1)S(1)}, bf16[128,2048]{1,0:T(8,128)(2,1)}, u32[]{:S(2)}) copy-start(bf16[128,2048]{1,0:T(8,128)(2,1)} %fusion.43) | copy-start | bytes 1572868
  135.2 57.0 %all-gather.6.cloned.1.call-start = ((), (), s32[]{:S(2)}) async-start(), calls=%async_computation.5 | async-start | bytes 2621440 | tf_op jit(solution)/shard_map/all_gather | solution.py:130
  135.9 204.5 %all-reduce.2.cloned.1.call-start = ((), (), s32[]{:S(2)}) async-start(), calls=%async_computation.7 | async-start | bytes 393216 | tf_op jit(solution)/shard_map/psum | solution.py:140
  196.7 156.6 %copy-start.4 = (bf16[128,2048]{1,0:T(8,128)(2,1)}, bf16[128,2048]{1,0:T(8,128)(2,1)S(1)}, u32[]{:S(2)}) copy-start(bf16[128,2048]{1,0:T(8,128)(2,1)S(1)} %fusion.26) | copy-start | bytes 1572868
Sparse Core Ops, SparseCore 0:
  12.4 75.2 all-gather.3
  89.4 30.1 all-gather.7
  137.8 31.9 all-gather.5
Sparse Core Ops, SparseCore 1:
  55.5 47.0 reduce-scatter.1
  197.7 142.7 all-reduce.1
